TPU v7x, 32 devices: a whole 2x2x4 slice. The times are simulated.
32 devices in a mesh: wide: 8 (over y, x, core), narrow: 4 (over z).
Axes of the slice: x: 2, y: 2, z: 4, core: 2. Of those that a mesh axis runs over, the one named last changes fastest.
Arguments:
- tokens: bfloat16 [32768, 512], P('wide'), may hold values from -6 to 6
- cotangent: bfloat16 [32768, 512], P('wide'), may hold values from -6 to 6
- segment_ids: int32 [8, 4096], P('wide'), may hold values from 0 to 3, never falling along the last dimension, each value on 1 to 2560 neighbouring positions
- pad_mask: int32 [8, 4096], P('wide'), may hold values 0 or 1
- owner_order: int32 [192], replicated, may hold values from 0 to 191, as said below
- weights: float32 [4, 192, 64, 64], P('narrow', 'wide')
- first_moment: float32 [4, 192, 64, 64], P('narrow', 'wide')
- second_moment: float32 [4, 192, 64, 64], P('narrow', 'wide'), as said below
- average: float32 [4, 192, 64, 64], P('narrow', 'wide')
- stats: float32 [4, 192, 2, 64, 64], P('narrow', 'wide'), as said below
- bases: float32 [4, 192, 2, 64, 64], P('narrow', 'wide'), as said below
- gains: float32 [1024], P('wide'), may hold values from 0.5 to 1.5
- gain_first: float32 [1024], P('wide'), may hold values from -128 to 128
- gain_second: float32 [1024], P('wide'), may hold values from 1723.5968 to 6881.28
- gain_average: float32 [1024], P('wide'), may hold values from 0.5 to 1.5
Outputs:
- output: bfloat16 [32768, 512], P('wide')
- input_grad: float32 [32768, 512], P('wide')
- new_weights: float32 [4, 192, 64, 64], P('narrow', 'wide')
- new_first: float32 [4, 192, 64, 64], P('narrow', 'wide')
- new_second: float32 [4, 192, 64, 64], P('narrow', 'wide')
- new_average: float32 [4, 192, 64, 64], P('narrow', 'wide')
- new_stats: float32 [4, 192, 2, 64, 64], P('narrow', 'wide')
- new_bases: float32 [4, 192, 2, 64, 64], P('narrow', 'wide')
- new_gains: float32 [1024], P('wide')
- gain_moment: float32 [1024], P('wide')
- gain_square: float32 [1024], P('wide')
- gain_mean: float32 [1024], P('wide')
Inputs may be any that keep to these rules, and one draw needn't show every extreme that they name: `segment_ids`: within a row segment numbers never fall; a segment holds at most 2560 positions. `owner_order`: each block number appears exactly once. `second_moment`: Positive. `stats`: each matrix is symmetric positive definite. `bases`: each matrix is orthogonal.
All inputs are finite; a program needn't handle non-finite values. No bound on the sum of `pad_mask` on one device may be relied on, other than what follows from the above.
Results may differ from a plain program's by a relative error of at most 0.025.
Values may be sent and summed in bfloat16 or wider, within the bound.
A program may use at most 192 MiB of HBM per device.

v0:
```python
from functools import partial
import jax
import jax.numpy as jnp
from jax import lax
from jax.sharding import PartitionSpec as P

HEADS = 8
HD = 64
FF = 2048
beta_one = 0.9
beta_two = 0.95
step_rate = 0.1
gain_rate = 0.75
weight_decay = 0.01
average_keep = 0.5
norm_eps = 1e-05
step_eps = 1e-08
masked_score = -1e30
highest = lax.Precision.HIGHEST


def normalize(values):
    center = jnp.mean(values, axis=-1, keepdims=True)
    centered = values - center
    variance = jnp.mean(centered * centered, axis=-1, keepdims=True)
    return centered * lax.rsqrt(variance + norm_eps)


def scaled_norm(values, gain):
    return normalize(values) * gain


def exact_gelu(values):
    return jax.nn.gelu(values, approximate=False)


def assemble(blocks, rows, cols):
    size = blocks.shape[-1]
    grid = blocks.reshape(rows // size, cols // size, size, size)
    return grid.transpose(0, 2, 1, 3).reshape(rows, cols)


def to_blocks(matrix, size):
    rows, cols = matrix.shape
    return (
        matrix.reshape(rows // size, size, cols // size, size)
        .transpose(0, 2, 1, 3)
        .reshape(-1, size, size)
    )


def masked_scores(query_rows, key_rows, seg_row, pad_row, block, scale, index):
    start = index * block
    query_block = lax.dynamic_slice_in_dim(query_rows, start, block, 0)
    query_pos = start + jnp.arange(block, dtype=jnp.int32)
    query_seg = lax.dynamic_slice_in_dim(seg_row, start, block, 0)
    positions = jnp.arange(seg_row.shape[0], dtype=jnp.int32)
    allowed = (query_seg[:, None] == seg_row[None, :]) & (
        (pad_row[None, :] == 1) | (query_pos[:, None] == positions[None, :])
    )
    scores = (
        jnp.einsum("qhd,khd->hqk", query_block, key_rows, preferred_element_type=jnp.float32)
        * scale
    )
    return (query_block, jnp.where(allowed[None], scores, masked_score))


def attend_forward(query_rows, key_rows, value_rows, seg_row, pad_row, block, scale, index):
    _, masked = masked_scores(query_rows, key_rows, seg_row, pad_row, block, scale, index)
    peak = jnp.max(masked, axis=-1, keepdims=True)
    total = peak + jnp.log(jnp.sum(jnp.exp(masked - peak), axis=-1, keepdims=True))
    probs = jnp.exp(masked - total).astype(jnp.bfloat16)
    attended = jnp.einsum("hqk,khd->qhd", probs, value_rows, preferred_element_type=jnp.float32)
    return (attended, total[..., 0])


def attend_backward(
    query_rows,
    key_rows,
    value_rows,
    seg_row,
    pad_row,
    back_attended,
    block,
    scale,
    carry,
    step_inputs,
):
    back_keys, back_values = carry
    index, total = step_inputs
    query_block, masked = masked_scores(query_rows, key_rows, seg_row, pad_row, block, scale, index)
    probs = jnp.exp(masked - total[:, :, None])
    probs_low = probs.astype(jnp.bfloat16)
    back_block = lax.dynamic_slice_in_dim(back_attended, index * block, block, 0)
    back_values = back_values + jnp.einsum(
        "hqk,qhd->khd", probs_low, back_block, preferred_element_type=jnp.float32
    )
    back_probs = jnp.einsum(
        "qhd,khd->hqk", back_block, value_rows, preferred_element_type=jnp.float32
    )
    back_scores = (
        probs * (back_probs - jnp.sum(probs * back_probs, axis=-1, keepdims=True))
    ).astype(jnp.bfloat16)
    back_query = (
        jnp.einsum("hqk,khd->qhd", back_scores, key_rows, preferred_element_type=jnp.float32)
        * scale
    )
    back_keys = (
        back_keys
        + jnp.einsum("hqk,qhd->khd", back_scores, query_block, preferred_element_type=jnp.float32)
        * scale
    )
    return ((back_keys, back_values), back_query)


def orthonormal(matrix):
    gram = jnp.einsum("...ji,...jk->...ik", matrix, matrix, precision=highest)
    lower = jnp.linalg.cholesky(gram)
    solved = jax.scipy.linalg.solve_triangular(lower, jnp.swapaxes(matrix, -1, -2), lower=True)
    return jnp.swapaxes(solved, -1, -2)


def soap_update(grad, weight, first, second, average, stats, bases):
    left = bases[..., 0, :, :]
    right = bases[..., 1, :, :]
    new_first = beta_one * first + (1.0 - beta_one) * grad
    rotated = jnp.einsum(
        "...ji,...jk->...ik",
        left,
        jnp.einsum("...jk,...kl->...jl", grad, right, precision=highest),
        precision=highest,
    )
    new_second = beta_two * second + (1.0 - beta_two) * rotated * rotated
    moment_rot = jnp.einsum(
        "...ji,...jk->...ik",
        left,
        jnp.einsum("...jk,...kl->...jl", new_first, right, precision=highest),
        precision=highest,
    )
    scaled = moment_rot / (jnp.sqrt(new_second) + step_eps)
    direction = jnp.einsum(
        "...ij,...jk->...ik",
        left,
        jnp.einsum("...jk,...lk->...jl", scaled, right, precision=highest),
        precision=highest,
    )
    new_weight = weight - step_rate * (direction + weight_decay * weight)
    new_average = average_keep * average + (1.0 - average_keep) * new_weight
    left_stat = beta_two * stats[..., 0, :, :] + (1.0 - beta_two) * jnp.einsum(
        "...ik,...jk->...ij", grad, grad, precision=highest
    )
    right_stat = beta_two * stats[..., 1, :, :] + (1.0 - beta_two) * jnp.einsum(
        "...ki,...kj->...ij", grad, grad, precision=highest
    )
    new_left = orthonormal(jnp.einsum("...ij,...jk->...ik", left_stat, left, precision=highest))
    new_right = orthonormal(jnp.einsum("...ij,...jk->...ik", right_stat, right, precision=highest))
    return (
        new_weight,
        new_first,
        new_second,
        new_average,
        jnp.stack([left_stat, right_stat], axis=-3),
        jnp.stack([new_left, new_right], axis=-3),
    )


def adam_gains(grad, gain, first, second, average):
    new_first = beta_one * first + (1.0 - beta_one) * grad
    new_second = beta_two * second + (1.0 - beta_two) * grad * grad
    new_gain = gain - gain_rate * new_first / (jnp.sqrt(new_second) + step_eps)
    new_average = average_keep * average + (1.0 - average_keep) * new_gain
    return (new_gain, new_first, new_second, new_average)


def body(
    tokens,
    cotangent,
    segment_ids,
    pad_mask,
    owner_order,
    weights,
    first_moment,
    second_moment,
    average,
    stats,
    bases,
    gains,
    gain_first,
    gain_second,
    gain_average,
):
    narrow = lax.axis_size("narrow")
    heads_here = HEADS // narrow
    units_here = FF // narrow
    span = heads_here * HD
    size = weights.shape[-1]
    width = tokens.shape[1]
    rows = tokens.shape[0]
    block_count = owner_order.shape[0]
    gathered, gain_all = (
        lax.all_gather(weights.astype(jnp.bfloat16), "wide", axis=1, tiled=True),
        lax.all_gather(gains.astype(jnp.bfloat16), "wide", axis=0, tiled=True),
    )
    slot_of = (
        jnp.zeros((block_count,), jnp.int32)
        .at[owner_order]
        .set(jnp.arange(block_count, dtype=jnp.int32))
    )
    blocks = gathered[0][slot_of]
    first_end = width // size * (3 * span // size)
    second_end = first_end + span // size * (width // size)
    third_end = second_end + width // size * (units_here // size)
    mixing = assemble(blocks[:first_end], width, 3 * span)
    out_weight = assemble(blocks[first_end:second_end], span, width)
    up_weight = assemble(blocks[second_end:third_end], width, units_here)
    down_weight = assemble(blocks[third_end:], units_here, width)
    gain_values = gain_all.astype(jnp.float32)
    gain_one = gain_values[:width]
    gain_two = gain_values[width:]
    seg_row = segment_ids[0]
    pad_row = pad_mask[0]
    pad_float = pad_row.astype(jnp.float32)
    inputs = tokens.astype(jnp.float32)
    normed_one = scaled_norm(inputs, gain_one).astype(jnp.bfloat16)
    mixed = jnp.dot(normed_one, mixing, preferred_element_type=jnp.float32).astype(jnp.bfloat16)
    query_rows = mixed[:, :span].reshape(rows, heads_here, HD)
    key_rows = mixed[:, span : 2 * span].reshape(rows, heads_here, HD)
    value_rows = mixed[:, 2 * span :].reshape(rows, heads_here, HD)
    block = min(512, rows)
    count = rows // block
    scale = HD ** (-0.5)
    forward_fn = partial(
        attend_forward, query_rows, key_rows, value_rows, seg_row, pad_row, block, scale
    )
    attended, totals = lax.map(forward_fn, jnp.arange(count, dtype=jnp.int32))
    attended = (
        (attended.reshape(rows, heads_here, HD) * pad_float[:, None, None])
        .astype(jnp.bfloat16)
        .reshape(rows, span)
    )
    branch_part = jnp.dot(attended, out_weight, preferred_element_type=jnp.float32)
    residual = inputs + lax.psum(branch_part.astype(jnp.bfloat16), "narrow").astype(jnp.float32)
    normed_full, second_back = jax.vjp(scaled_norm, residual, gain_two)
    normed_two = normed_full.astype(jnp.bfloat16)
    up = jnp.dot(normed_two, up_weight, preferred_element_type=jnp.float32)
    active_full, gelu_back = jax.vjp(exact_gelu, up)
    active = active_full.astype(jnp.bfloat16)
    down_part = jnp.dot(active, down_weight, preferred_element_type=jnp.float32)
    output = (
        residual + lax.psum(down_part.astype(jnp.bfloat16), "narrow").astype(jnp.float32)
    ).astype(jnp.bfloat16)
    grad_down = jnp.einsum("tf,td->fd", active, cotangent, preferred_element_type=jnp.float32)
    back_active = jnp.einsum(
        "td,fd->tf", cotangent, down_weight, preferred_element_type=jnp.float32
    )
    back_up = gelu_back(back_active)[0].astype(jnp.bfloat16)
    grad_up = jnp.einsum("td,tf->df", normed_two, back_up, preferred_element_type=jnp.float32)
    back_normed_two = jnp.einsum(
        "tf,df->td", back_up, up_weight, preferred_element_type=jnp.float32
    )
    back_two_full = lax.psum(back_normed_two.astype(jnp.bfloat16), "narrow").astype(jnp.float32)
    from_norm, grad_gain_two = second_back(back_two_full)
    back_residual = cotangent.astype(jnp.float32) + from_norm
    back_branch = back_residual.astype(jnp.bfloat16)
    grad_out = jnp.einsum("tc,td->cd", attended, back_branch, preferred_element_type=jnp.float32)
    back_attended = jnp.einsum(
        "td,cd->tc", back_branch, out_weight, preferred_element_type=jnp.float32
    ).astype(jnp.bfloat16)
    back_attended = (back_attended * pad_row.astype(jnp.bfloat16)[:, None]).reshape(
        rows, heads_here, HD
    )
    backward_fn = partial(
        attend_backward,
        query_rows,
        key_rows,
        value_rows,
        seg_row,
        pad_row,
        back_attended,
        block,
        scale,
    )
    zeros_rows = jnp.zeros((rows, heads_here, HD), jnp.float32)
    (back_keys, back_values), back_queries = lax.scan(
        backward_fn, (zeros_rows, zeros_rows), (jnp.arange(count, dtype=jnp.int32), totals)
    )
    back_mixed = jnp.concatenate(
        [
            back_queries.reshape(rows, span),
            back_keys.reshape(rows, span),
            back_values.reshape(rows, span),
        ],
        axis=1,
    ).astype(jnp.bfloat16)
    grad_mixing = jnp.einsum(
        "td,tc->dc", normed_one, back_mixed, preferred_element_type=jnp.float32
    )
    back_normed_one = jnp.einsum(
        "tc,dc->td", back_mixed, mixing, preferred_element_type=jnp.float32
    )
    back_one_full = lax.psum(back_normed_one.astype(jnp.bfloat16), "narrow").astype(jnp.float32)
    _, first_back = jax.vjp(scaled_norm, inputs, gain_one)
    from_first, grad_gain_one = first_back(back_one_full)
    input_grad = back_residual + from_first
    gain_grad = jnp.concatenate([grad_gain_one, grad_gain_two])
    grad_blocks = jnp.concatenate(
        [
            to_blocks(grad_mixing, size),
            to_blocks(grad_out, size),
            to_blocks(grad_up, size),
            to_blocks(grad_down, size),
        ],
        axis=0,
    )
    slot_grads = grad_blocks[owner_order]
    own_grad, own_gain_grad = (
        lax.psum_scatter(
            slot_grads.astype(jnp.bfloat16), "wide", scatter_dimension=0, tiled=True
        ).astype(jnp.float32),
        lax.psum_scatter(
            gain_grad.astype(jnp.bfloat16), "wide", scatter_dimension=0, tiled=True
        ).astype(jnp.float32),
    )
    new_weight, new_first, new_second, new_average, new_stats, new_bases = soap_update(
        own_grad[None], weights, first_moment, second_moment, average, stats, bases
    )
    new_gains, gain_moment, gain_square, gain_mean = adam_gains(
        own_gain_grad, gains, gain_first, gain_second, gain_average
    )
    return (
        output,
        input_grad,
        new_weight,
        new_first,
        new_second,
        new_average,
        new_stats,
        new_bases,
        new_gains,
        gain_moment,
        gain_square,
        gain_mean,
    )


def solution(mesh):
    placed = (
        P("wide", None),
        P("wide", None),
        P("wide", None),
        P("wide", None),
        P(),
        P("narrow", "wide", None, None),
        P("narrow", "wide", None, None),
        P("narrow", "wide", None, None),
        P("narrow", "wide", None, None),
        P("narrow", "wide", None, None, None),
        P("narrow", "wide", None, None, None),
        P("wide"),
        P("wide"),
        P("wide"),
        P("wide"),
    )
    return jax.shard_map(
        body,
        mesh=mesh,
        in_specs=placed,
        out_specs=(
            P("wide", None),
            P("wide", None),
            P("narrow", "wide", None, None),
            P("narrow", "wide", None, None),
            P("narrow", "wide", None, None),
            P("narrow", "wide", None, None),
            P("narrow", "wide", None, None, None),
            P("narrow", "wide", None, None, None),
            P("wide"),
            P("wide"),
            P("wide"),
            P("wide"),
        ),
        check_vma=False,
    )
```

profile of v0, /device:TPU:0, one launch (start us, length us, event | category | flops | bytes accessed | tf_op | source)
XLA Modules:
  0.0 1682.4 jit_solution(14273510150274380255)
XLA Ops:
  12.6 10.2 all-gather
  29.7 15.9 all-gather.3.cloned.1.call-done
  60.9 140.6 %while.29 = (s32[]{:T(128)}, f32[8,512,2,64]{1,3,2,0:T(8,128)}, f32[8,2,512]{2,1,0:T(2,128)S(1)}, s32[8]{0:T(128)S(1)}, s32[4096]{0:T(1024)S(1)}, /*index=5*/s32...) while((s32[]{:T(128)}, f32[8,512,2,64]{1,3,2,0:T(8,128)}, ...), condition=%wide.region_6.7_spmd.clone, body=%wide.region_3.6_spmd.sunk.clone | while | flops 1128271360 | bytes 61294784 | solution.py:235
  73.8 5.0 fusion.215
  91.3 5.0 fusion.215
  104.3 4.6 exponential_reduce_fusion.3
  108.9 5.0 fusion.215
  121.8 4.6 exponential_reduce_fusion.3
  126.4 5.0 fusion.215
  143.9 4.9 fusion.215
  161.5 4.9 fusion.215
  179.0 4.9 fusion.215
  196.5 5.0 fusion.215
  214.2 149.3 %all-reduce.6.cloned.1.call-done = bf16[4096,512]{1,0:T(8,128)(2,1)} async-done(((bf16[4096,512]{1,0:T(8,128)(2,1)}), bf16[4096,512]{1,0:T(8,128)(2,1)}) %all-reduce.6.cloned.1.call-update) | async-done | bytes 4194320 | tf_op jit(solution)/shard_map/psum | solution.py:242
  363.6 4.8 fusion.68
  374.0 20.7 %multiply_convert_fusion.1 = (bf16[4096,512]{1,0:T(8,128)(2,1)}, f32[4096,512]{1,0:T(8,128)S(1)}, f32[4096,512]{1,0:T(8,128)}) fusion(bf16[4096,512]{1,0:T(8,128)(2,1)S(1)} %multiply_convert_fusion.2, bf16[512,512]{1,0:T(8,128)(2,1)S(1)} %reshape.466), kind=kOutput, calls=%fused_computation.92 | convolution fusion | flops 2283798528 | bytes 25690112 | tf_op jit(solution)/shard_map/dot_general | solution.py:245
  394.7 6.4 fusion.60
  424.0 6.6 fusion.128
  435.5 126.2 %all-reduce.8.cloned.1.call-done = bf16[4096,512]{1,0:T(8,128)(2,1)} async-done(((bf16[4096,512]{1,0:T(8,128)(2,1)}), bf16[4096,512]{1,0:T(8,128)(2,1)}) %all-reduce.8.cloned.1.call-update) | async-done | bytes 4194320 | tf_op jit(solution)/shard_map/psum | solution.py:261
  561.7 9.3 fusion.50
  581.1 416.0 %while.30 = (s32[]{:T(128)}, f32[4096,2,64]{0,2,1:T(8,128)S(1)}, f32[4096,2,64]{0,2,1:T(8,128)}, bf16[8,512,2,64]{1,3,2,0:T(8,128)(2,1)}, s32[8]{0:T(128)S(1)}, ...) while((s32[]{:T(128)}, f32[4096,2,64]{0,2,1:T(8,128)S(1)}, ...), condition=%wide.region_16.17_spmd.clone.clone, body=%wide.region_14.16_spmd.clone.sunk.clone | while | flops 2758348288 | bytes 217921824 | solution.py:284
  589.0 5.7 copy-done
  594.8 7.3 fusion.228
  602.0 12.7 multiply_reduce_fusion.4
  614.7 12.3 multiply_convert_fusion.7
  640.6 5.7 copy-done
  646.3 7.6 fusion.228
  654.0 12.7 multiply_reduce_fusion.4
  666.7 12.3 multiply_convert_fusion.7
  692.6 5.7 copy-done
  698.3 7.6 fusion.228
  706.0 12.7 multiply_reduce_fusion.4
  718.7 12.3 multiply_convert_fusion.7
  744.6 5.7 copy-done
  750.3 7.6 fusion.228
  757.9 12.7 multiply_reduce_fusion.4
  770.7 12.3 multiply_convert_fusion.7
  796.6 5.7 copy-done
  802.3 7.6 fusion.228
  809.9 12.7 multiply_reduce_fusion.4
  822.6 12.3 multiply_convert_fusion.7
  848.5 5.7 copy-done
  854.2 7.6 fusion.228
  861.9 12.7 multiply_reduce_fusion.4
  874.6 12.3 multiply_convert_fusion.7
  900.5 5.7 copy-done
  906.2 7.6 fusion.228
  913.9 12.7 multiply_reduce_fusion.4
  926.6 12.3 multiply_convert_fusion.7
  952.5 5.7 copy-done
  958.2 7.6 fusion.228
  965.8 12.7 multiply_reduce_fusion.4
  978.6 12.3 multiply_convert_fusion.7
  1005.0 6.4 copy.155
  1019.6 6.8 convolution_convert_fusion.3
  1045.6 19.3 %reduce-scatter.2.cloned.1.call-done = bf16[24,64,64]{2,1,0:T(8,128)(2,1)} async-done(((bf16[192,64,64]{2,1,0:T(8,128)(2,1)}), bf16[24,64,64]{2,1,0:T(8,128)(2,1)}) %reduce-scatter.2.cloned.1.call-update) | async-done | bytes 196624 | tf_op jit(solution)/shard_map/reduce_scatter | solution.py:317
  1094.8 142.1 %custom-call.12 = f32[1,24,64,64]{3,2,1,0:T(8,128)} custom-call(f32[1,24,64,64]{3,2,1,0:T(8,128)} %fusion.96), custom_call_target="Cholesky" | custom-call | tf_op jit(solution)/shard_map/jit(cholesky)/cholesky | solution.py:118
  1242.5 142.3 %custom-call.10 = f32[1,24,64,64]{3,2,1,0:T(8,128)} custom-call(f32[1,24,64,64]{3,2,1,0:T(8,128)} %fusion.98), custom_call_target="Cholesky" | custom-call | tf_op jit(solution)/shard_map/jit(cholesky)/cholesky | solution.py:118
  1389.2 119.3 %custom-call.11 = f32[24,1,64,64]{2,3,1,0:T(8,128)} custom-call(f32[24,1,64,64]{3,2,1,0:T(8,128)} %get-tuple-element.308), custom_call_target="InvertDiagBlocksLowerTriangular" | custom-call | tf_op jit(solution)/shard_map/jit(_solve_triangular)/vmap()/triangular_solve | solution.py:119
  1508.6 119.3 %custom-call.13 = f32[24,1,64,64]{2,3,1,0:T(8,128)} custom-call(f32[24,1,64,64]{3,2,1,0:T(8,128)} %get-tuple-element.309), custom_call_target="InvertDiagBlocksLowerTriangular" | custom-call | tf_op jit(solution)/shard_map/jit(_solve_triangular)/vmap()/triangular_solve | solution.py:119
  1636.8 5.9 fusion.53
  1642.8 4.7 fusion.51
  1647.6 12.8 all-reduce
  1661.0 14.7 add_add_fusion.2
  (410 shorter events, 356.4 us)
Async XLA Ops:
  7.2 38.3 %all-gather.3.cloned.1.call-start = ((), (), s32[]{:S(2)}) async-start(), calls=%async_computation.1 | async-start | bytes 3538944 | tf_op jit(solution)/shard_map/all_gather | solution.py:201
  9.2 354.4 %all-reduce.6.cloned.1.call-start = ((), (), s32[]{:S(2)}) async-start(), calls=%async_computation.2 | async-start | bytes 8388608 | tf_op jit(solution)/shard_map/psum | solution.py:242
  10.7 12.1 copy-start.57
  22.8 33.7 %copy-start.51 = (f32[4,1,128]{2,1,0:T(1,128)}, f32[4,1,128]{2,1,0:T(1,128)S(1)}, u32[]{:S(2)}) copy-start(f32[4,1,128]{2,1,0:T(1,128)S(1)} %get-tuple-element.311) | copy-start | bytes 6148
  25.7 35.0 %copy-start.41 = (f32[4096]{0:T(1024)}, f32[4096]{0:T(1024)S(1)}, u32[]{:S(2)}) copy-start(f32[4096]{0:T(1024)S(1)} %broadcast_multiply_fusion.1) | copy-start | bytes 49156
  29.6 31.0 %copy-start.44 = (f32[4096]{0:T(1024)}, f32[4096]{0:T(1024)S(1)}, u32[]{:S(2)}) copy-start(f32[4096]{0:T(1024)S(1)} %fusion.110) | copy-start | bytes 49156
  48.6 7.9 copy-start.17
  201.5 7.0 copy-start.10
  208.5 353.2 %all-reduce.8.cloned.1.call-start = ((), (), s32[]{:S(2)}) async-start(), calls=%async_computation.3 | async-start | bytes 8388608 | tf_op jit(solution)/shard_map/psum | solution.py:261
  363.6 4.8 copy-start.1
  363.6 5.9 copy-start.5
  374.0 20.7 %copy-start.23 = (bf16[4096,512]{1,0:T(8,128)(2,1)}, bf16[4096,512]{1,0:T(8,128)(2,1)S(1)}, u32[]{:S(2)}) copy-start(bf16[4096,512]{1,0:T(8,128)(2,1)S(1)} %multiply_convert_fusion.2) | copy-start | bytes 12582916
  374.0 20.7 %copy-start.13 = (bf16[4096,512]{1,0:T(8,128)(2,1)S(1)}, bf16[4096,512]{1,0:T(8,128)(2,1)}, u32[]{:S(2)}) copy-start(bf16[4096,512]{1,0:T(8,128)(2,1)} %param.23) | copy-start | bytes 12582916
  374.0 20.7 %copy-start.40 = (bf16[512,512]{1,0:T(8,128)(2,1)S(1)}, bf16[512,512]{1,0:T(8,128)(2,1)}, u32[]{:S(2)}) copy-start(bf16[512,512]{1,0:T(8,128)(2,1)} %reshape.468) | copy-start | bytes 1572868
  403.1 4.7 copy-start.58
  407.6 657.4 %reduce-scatter.2.cloned.1.call-start = ((), (), s32[]{:S(2)}) async-start(), calls=%async_computation.4 | async-start | bytes 3538944 | tf_op jit(solution)/shard_map/reduce_scatter | solution.py:317
  407.8 8.1 copy-start.24
  407.8 8.1 copy-start.65
  561.7 9.4 copy-start.2
  561.7 9.4 copy-start.6
  561.7 9.4 copy-start.15
  589.0 5.7 copy-start
  594.7 7.3 copy-start.11
  640.6 5.7 copy-start
  646.3 7.7 copy-start.11
  692.6 5.7 copy-start
  698.3 7.7 copy-start.11
  744.6 5.7 copy-start
  750.3 7.7 copy-start.11
  796.5 5.7 copy-start
  802.3 7.7 copy-start.11
  848.5 5.7 copy-start
  854.2 7.7 copy-start.11
  900.5 5.7 copy-start
  906.2 7.7 copy-start.11
  952.5 5.7 copy-start
  958.2 7.7 copy-start.11
  1003.1 8.2 copy-start.33
  1011.3 4.5 copy-start.25
  1011.3 4.5 copy-start.26
  1011.3 4.5 copy-start.27
  1019.5 6.9 copy-start.35
  1019.5 6.9 copy-start.37
  1019.5 6.9 copy-start.39
  1019.5 6.9 copy-start.43
  1019.5 617.2 %all-reduce.10.cloned.1.call-start = ((), (), s32[]{:S(2)}) async-start(), calls=%async_computation.5 | async-start | bytes 16777216 | tf_op jit(solution)/shard_map/psum | solution.py:250
  1030.8 12.4 copy-start.63
  1030.8 34.2 %copy-start.12 = (f32[1,24,2,64,64]{4,3,2,1,0:T(8,128)S(1)}, f32[1,24,2,64,64]{4,3,2,1,0:T(8,128)}, u32[]{:S(2)}) copy-start(f32[1,24,2,64,64]{4,3,2,1,0:T(8,128)} %param.32) | copy-start | bytes 2359300
  1074.3 12.0 copy-start.16
  1238.4 146.4 %copy-start.55 = (pred[64,64]{1,0:T(8,128)(4,1)S(1)}, pred[64,64]{1,0:T(8,128)(4,1)}, u32[]{:S(2)}) copy-start(pred[64,64]{1,0:T(8,128)(4,1)} %iota_compare_fusion.3) | copy-start | bytes 12292
  1238.4 148.1 %copy-start.54 = (pred[64,64]{1,0:T(8,128)(4,1)S(1)}, pred[64,64]{1,0:T(8,128)(4,1)}, u32[]{:S(2)}) copy-start(pred[64,64]{1,0:T(8,128)(4,1)} %iota_compare_fusion.2) | copy-start | bytes 12292
  1242.5 392.4 %copy-start.19 = (f32[24,64,64]{1,2,0:T(8,128)S(1)}, f32[24,64,64]{1,2,0:T(8,128)}, u32[]{:S(2)}) copy-start(f32[24,64,64]{1,2,0:T(8,128)} %copy-done.18) | copy-start | bytes 1179652
  1242.5 392.4 %copy-start.21 = (f32[24,64,64]{1,2,0:T(8,128)S(1)}, f32[24,64,64]{1,2,0:T(8,128)}, u32[]{:S(2)}) copy-start(f32[24,64,64]{1,2,0:T(8,128)} %copy-done.20) | copy-start | bytes 1179652
  1630.5 6.2 copy-start.53
  1633.3 9.4 copy-start.50
  1633.3 9.5 copy-start.46
  1636.7 6.0 copy-start.4
  1636.7 6.0 copy-start.9
  1636.8 10.8 copy-start.56
  1636.8 23.6 %copy-start.59 = (f32[128]{0:T(128)S(1)}, f32[128]{0:T(128)}, u32[]{:S(2)}) copy-start(f32[128]{0:T(128)} %param.33) | copy-start | bytes 1540
  1636.8 23.6 %copy-start.60 = (f32[128]{0:T(128)S(1)}, f32[128]{0:T(128)}, u32[]{:S(2)}) copy-start(f32[128]{0:T(128)} %param.36) | copy-start | bytes 1540
  1636.8 23.6 %copy-start.61 = (f32[128]{0:T(128)S(1)}, f32[128]{0:T(128)}, u32[]{:S(2)}) copy-start(f32[128]{0:T(128)} %param.34) | copy-start | bytes 1540
  1636.8 23.6 %copy-start.62 = (f32[128]{0:T(128)S(1)}, f32[128]{0:T(128)}, u32[]{:S(2)}) copy-start(f32[128]{0:T(128)} %param.35) | copy-start | bytes 1540
  1636.8 24.2 %copy-start.48 = (f32[4096]{0:T(1024)S(1)}, f32[4096]{0:T(1024)}, u32[]{:S(2)}) copy-start(f32[4096]{0:T(1024)} %copy-done.47) | copy-start | bytes 49156
  (21 other events, 54.6 us)
Sparse Core Ops, SparseCore 0:
  10.5 35.0 all-gather.2
  208.6 154.9 all-reduce.5
  407.7 153.9 all-reduce.7
  1019.6 45.2 reduce-scatter.1
  1068.1 291.6 all-reduce.9
where the time goes:
time: 1690 us; the launch traced here: 1680 us
  other arithmetic  782 us (46%)
  matrix products  401 us (24%)
  waiting for transfers between devices  311 us (18%)
  local copies, waits for them, and re-layouts  137 us (8%)
  blocking collectives  23 us (1%)
    another operation x5, other arithmetic, orthonormal(): lower = jnp.linalg.cholesky(gram)  287 us
    another operation x4, other arithmetic, orthonormal(): jax.scipy.linalg.solve_triangular(lower, jnp.swapaxes(matrix, -1, -2), lo...  242 us
    psum x1, waiting for transfers between devices, body(): lax.psum(branch_part.astype(jnp.bfloat16), 'narrow').astype(jnp.float32)  149 us
    psum x1, waiting for transfers between devices, body(): lax.psum(back_normed_two.astype(jnp.bfloat16), 'narrow').astype(jnp.float32)  126 us
    dot_general x8, matrix products, attend_backward(): jnp.einsum('qhd,khd->hqk', back_block, value_rows, preferred_element_type...  102 us
    convert_element_type x8, other arithmetic, attend_backward(): back_scores = (probs * (back_probs - jnp.sum(probs * back_probs, axis=-1,...  98.3 us
    dot_general x8, matrix products, attend_backward(): jnp.einsum('hqk,qhd->khd', probs_low, back_block, preferred_element_type=...  60.8 us
    dot_general x16, matrix products, masked_scores(): jnp.einsum('qhd,khd->hqk', query_block, key_rows, preferred_element_type=...  56.2 us
  transfers between devices with their start and end apart: 5, of which 4 were waited for; matrix products, arithmetic and copies ran while one was open for 38% of the time, Pallas kernels for 0%

commit v1 on v0

--- a/solution.py
+++ b/solution.py
@@ -258,7 +258,9 @@
     back_normed_two = jnp.einsum(
         "tf,df->td", back_up, up_weight, preferred_element_type=jnp.float32
     )
-    back_two_full = lax.psum(back_normed_two.astype(jnp.bfloat16), "narrow").astype(jnp.float32)
+    back_two_full = jnp.sum(
+        lax.all_gather(back_normed_two.astype(jnp.bfloat16), "narrow"), axis=0
+    ).astype(jnp.float32)
     from_norm, grad_gain_two = second_back(back_two_full)
     back_residual = cotangent.astype(jnp.float32) + from_norm
     back_branch = back_residual.astype(jnp.bfloat16)

time: 1690 us -> 1830 us (1.083)
  waiting for transfers between devices: 311 us -> 441 us
    all_gather x0 -> x1, waiting for transfers between devices: none -> 257 us  [body(): lax.all_gather(back_normed_two.astype(jnp.bfloat16), 'narrow')]
    psum x1 -> x0, waiting for transfers between devices: 126 us -> none  [body(): lax.psum(back_normed_two.astype(jnp.bfloat16), 'narrow').astype(jnp.float32)]
  transfers between devices with their start and end apart: 5 -> 5, of which waited for: 4 -> 4; matrix products, arithmetic and copies ran while one was open for 38% -> 35% of each run, Pallas kernels for 0% -> 0%
where the time goes in v1:
time: 1830 us
  other arithmetic  794 us (43%)
  waiting for transfers between devices  441 us (24%)
  matrix products  402 us (22%)
  local copies, waits for them, and re-layouts  137 us (7%)
  blocking collectives  22.9 us (1%)
    another operation x5, other arithmetic, orthonormal(): lower = jnp.linalg.cholesky(gram)  287 us
    all_gather x1, waiting for transfers between devices, body(): lax.all_gather(back_normed_two.astype(jnp.bfloat16), 'narrow')  257 us
    another operation x4, other arithmetic, orthonormal(): jax.scipy.linalg.solve_triangular(lower, jnp.swapaxes(matrix, -1, -2), lo...  242 us
    psum x1, waiting for transfers between devices, body(): lax.psum(branch_part.astype(jnp.bfloat16), 'narrow').astype(jnp.float32)  149 us
    dot_general x8, matrix products, attend_backward(): jnp.einsum('qhd,khd->hqk', back_block, value_rows, preferred_element_type...  102 us
    convert_element_type x8, other arithmetic, attend_backward(): back_scores = (probs * (back_probs - jnp.sum(probs * back_probs, axis=-1,...  98.3 us
    dot_general x8, matrix products, attend_backward(): jnp.einsum('hqk,qhd->khd', probs_low, back_block, preferred_element_type=...  60.8 us
    dot_general x16, matrix products, masked_scores(): jnp.einsum('qhd,khd->hqk', query_block, key_rows, preferred_element_type=...  56.2 us
  transfers between devices with their start and end apart: 5, of which 4 were waited for; matrix products, arithmetic and copies ran while one was open for 35% of the time, Pallas kernels for 0%

profile of v1, /device:TPU:0, one launch (start us, length us, event | category | flops | bytes accessed | tf_op | source)
XLA Modules:
  0.0 1825.3 jit_solution(12305392036439251481)
XLA Ops:
  12.6 10.2 all-gather.1
  29.7 15.9 all-gather.5.cloned.1.call-done
  60.9 140.6 %while.29 = (s32[]{:T(128)}, f32[8,512,2,64]{1,3,2,0:T(8,128)}, f32[8,2,512]{2,1,0:T(2,128)S(1)}, s32[8]{0:T(128)S(1)}, s32[4096]{0:T(1024)S(1)}, /*index=5*/s32...) while((s32[]{:T(128)}, f32[8,512,2,64]{1,3,2,0:T(8,128)}, ...), condition=%wide.region_6.7_spmd.clone, body=%wide.region_3.6_spmd.sunk.clone | while | flops 1128271360 | bytes 61294784 | solution.py:235
  73.8 5.0 fusion.215
  91.3 5.0 fusion.215
  104.3 4.6 exponential_reduce_fusion.3
  108.9 5.0 fusion.215
  126.4 5.0 fusion.215
  143.9 4.9 fusion.215
  161.5 4.9 fusion.215
  179.0 4.9 fusion.215
  196.5 5.0 fusion.215
  214.2 149.3 %all-reduce.5.cloned.1.call-done = bf16[4096,512]{1,0:T(8,128)(2,1)} async-done(((bf16[4096,512]{1,0:T(8,128)(2,1)}), bf16[4096,512]{1,0:T(8,128)(2,1)}) %all-reduce.5.cloned.1.call-update) | async-done | bytes 4194320 | tf_op jit(solution)/shard_map/psum | solution.py:242
  363.6 4.8 fusion.68
  374.0 20.7 %multiply_convert_fusion.1 = (bf16[4096,512]{1,0:T(8,128)(2,1)}, f32[4096,512]{1,0:T(8,128)S(1)}, f32[4096,512]{1,0:T(8,128)}) fusion(bf16[4096,512]{1,0:T(8,128)(2,1)S(1)} %multiply_convert_fusion.2, bf16[512,512]{1,0:T(8,128)(2,1)S(1)} %reshape.466), kind=kOutput, calls=%fused_computation.92 | convolution fusion | flops 2283798528 | bytes 25690112 | tf_op jit(solution)/shard_map/dot_general | solution.py:245
  394.7 6.4 fusion.60
  424.2 7.1 fusion.128
  436.1 257.4 %all-gather.7.cloned.1.call-done = bf16[16384,512]{1,0:T(8,128)(2,1)} async-done(((bf16[4096,512]{1,0:T(8,128)(2,1)}), bf16[16384,512]{1,0:T(8,128)(2,1)}) %all-gather.7.cloned.1.call-update) | async-done | bytes 16777232 | tf_op jit(solution)/shard_map/all_gather | solution.py:262
  693.5 11.8 reduce_sum.128
  705.4 9.4 fusion.50
  724.9 416.0 %while.30 = (s32[]{:T(128)}, f32[4096,2,64]{0,2,1:T(8,128)S(1)}, f32[4096,2,64]{0,2,1:T(8,128)}, bf16[8,512,2,64]{1,3,2,0:T(8,128)(2,1)}, s32[8]{0:T(128)S(1)}, ...) while((s32[]{:T(128)}, f32[4096,2,64]{0,2,1:T(8,128)S(1)}, ...), condition=%wide.region_16.17_spmd.clone.clone, body=%wide.region_14.16_spmd.clone.sunk.clone | while | flops 2758348288 | bytes 217921824 | solution.py:286
  732.8 5.7 copy-done
  738.5 7.3 fusion.228
  745.8 12.7 multiply_reduce_fusion.4
  758.5 12.3 multiply_convert_fusion.7
  784.4 5.7 copy-done
  790.1 7.6 fusion.228
  797.8 12.7 multiply_reduce_fusion.4
  810.5 12.3 multiply_convert_fusion.7
  836.4 5.7 copy-done
  842.1 7.6 fusion.228
  849.7 12.7 multiply_reduce_fusion.4
  862.4 12.3 multiply_convert_fusion.7
  888.3 5.7 copy-done
  894.1 7.6 fusion.228
  901.7 12.7 multiply_reduce_fusion.4
  914.4 12.3 multiply_convert_fusion.7
  940.3 5.7 copy-done
  946.0 7.6 fusion.228
  953.7 12.7 multiply_reduce_fusion.4
  966.4 12.3 multiply_convert_fusion.7
  992.3 5.7 copy-done
  998.0 7.6 fusion.228
  1005.7 12.7 multiply_reduce_fusion.4
  1018.4 12.3 multiply_convert_fusion.7
  1044.3 5.7 copy-done
  1050.0 7.6 fusion.228
  1057.6 12.7 multiply_reduce_fusion.4
  1070.3 12.3 multiply_convert_fusion.7
  1096.2 5.7 copy-done
  1102.0 7.6 fusion.228
  1109.6 12.7 multiply_reduce_fusion.4
  1122.3 12.3 multiply_convert_fusion.7
  1148.7 6.4 copy.155
  1163.3 6.8 convolution_convert_fusion.3
  1189.5 18.4 %reduce-scatter.2.cloned.1.call-done = bf16[24,64,64]{2,1,0:T(8,128)(2,1)} async-done(((bf16[192,64,64]{2,1,0:T(8,128)(2,1)}), bf16[24,64,64]{2,1,0:T(8,128)(2,1)}) %reduce-scatter.2.cloned.1.call-update) | async-done | bytes 196624 | tf_op jit(solution)/shard_map/reduce_scatter | solution.py:319
  1237.8 142.1 %custom-call.12 = f32[1,24,64,64]{3,2,1,0:T(8,128)} custom-call(f32[1,24,64,64]{3,2,1,0:T(8,128)} %fusion.96), custom_call_target="Cholesky" | custom-call | tf_op jit(solution)/shard_map/jit(cholesky)/cholesky | solution.py:118
  1385.5 142.3 %custom-call.10 = f32[1,24,64,64]{3,2,1,0:T(8,128)} custom-call(f32[1,24,64,64]{3,2,1,0:T(8,128)} %fusion.98), custom_call_target="Cholesky" | custom-call | tf_op jit(solution)/shard_map/jit(cholesky)/cholesky | solution.py:118
  1532.2 119.3 %custom-call.11 = f32[24,1,64,64]{2,3,1,0:T(8,128)} custom-call(f32[24,1,64,64]{3,2,1,0:T(8,128)} %get-tuple-element.308), custom_call_target="InvertDiagBlocksLowerTriangular" | custom-call | tf_op jit(solution)/shard_map/jit(_solve_triangular)/vmap()/triangular_solve | solution.py:119
  1651.6 119.3 %custom-call.13 = f32[24,1,64,64]{2,3,1,0:T(8,128)} custom-call(f32[24,1,64,64]{3,2,1,0:T(8,128)} %get-tuple-element.309), custom_call_target="InvertDiagBlocksLowerTriangular" | custom-call | tf_op jit(solution)/shard_map/jit(_solve_triangular)/vmap()/triangular_solve | solution.py:119
  1779.8 5.9 fusion.53
  1785.8 4.7 fusion.51
  1790.6 12.7 all-reduce
  1804.0 14.7 add_add_fusion.2
  (411 shorter events, 361.2 us)
Async XLA Ops:
  7.2 38.3 %all-gather.5.cloned.1.call-start = ((), (), s32[]{:S(2)}) async-start(), calls=%async_computation.1 | async-start | bytes 3538944 | tf_op jit(solution)/shard_map/all_gather | solution.py:201
  9.2 354.4 %all-reduce.5.cloned.1.call-start = ((), (), s32[]{:S(2)}) async-start(), calls=%async_computation.2 | async-start | bytes 8388608 | tf_op jit(solution)/shard_map/psum | solution.py:242
  10.7 12.1 copy-start.57
  22.8 33.7 %copy-start.51 = (f32[4,1,128]{2,1,0:T(1,128)}, f32[4,1,128]{2,1,0:T(1,128)S(1)}, u32[]{:S(2)}) copy-start(f32[4,1,128]{2,1,0:T(1,128)S(1)} %get-tuple-element.311) | copy-start | bytes 6148
  25.7 35.0 %copy-start.41 = (f32[4096]{0:T(1024)}, f32[4096]{0:T(1024)S(1)}, u32[]{:S(2)}) copy-start(f32[4096]{0:T(1024)S(1)} %broadcast_multiply_fusion.1) | copy-start | bytes 49156
  29.6 31.0 %copy-start.44 = (f32[4096]{0:T(1024)}, f32[4096]{0:T(1024)S(1)}, u32[]{:S(2)}) copy-start(f32[4096]{0:T(1024)S(1)} %fusion.110) | copy-start | bytes 49156
  48.6 7.9 copy-start.17
  201.5 7.0 copy-start.10
  208.5 485.1 %all-gather.7.cloned.1.call-start = ((), (), s32[]{:S(2)}) async-start(), calls=%async_computation.4 | async-start | bytes 20971520 | tf_op jit(solution)/shard_map/all_gather | solution.py:262
  363.6 4.8 copy-start.1
  363.6 5.9 copy-start.5
  374.0 20.7 %copy-start.23 = (bf16[4096,512]{1,0:T(8,128)(2,1)}, bf16[4096,512]{1,0:T(8,128)(2,1)S(1)}, u32[]{:S(2)}) copy-start(bf16[4096,512]{1,0:T(8,128)(2,1)S(1)} %multiply_convert_fusion.2) | copy-start | bytes 12582916
  374.0 20.7 %copy-start.14 = (bf16[4096,512]{1,0:T(8,128)(2,1)S(1)}, bf16[4096,512]{1,0:T(8,128)(2,1)}, u32[]{:S(2)}) copy-start(bf16[4096,512]{1,0:T(8,128)(2,1)} %param.23) | copy-start | bytes 12582916
  374.0 20.7 %copy-start.40 = (bf16[512,512]{1,0:T(8,128)(2,1)S(1)}, bf16[512,512]{1,0:T(8,128)(2,1)}, u32[]{:S(2)}) copy-start(bf16[512,512]{1,0:T(8,128)(2,1)} %reshape.468) | copy-start | bytes 1572868
  403.2 4.7 copy-start.58
  407.6 800.3 %reduce-scatter.2.cloned.1.call-start = ((), (), s32[]{:S(2)}) async-start(), calls=%async_computation.3 | async-start | bytes 3538944 | tf_op jit(solution)/shard_map/reduce_scatter | solution.py:319
  407.9 8.1 copy-start.24
  407.9 8.1 copy-start.65
  705.4 9.4 copy-start.2
  705.4 9.5 copy-start.6
  705.4 9.5 copy-start.12
  732.8 5.7 copy-start
  738.5 7.3 copy-start.11
  784.4 5.7 copy-start
  790.1 7.7 copy-start.11
  836.4 5.7 copy-start
  842.1 7.7 copy-start.11
  888.3 5.7 copy-start
  894.1 7.7 copy-start.11
  940.3 5.7 copy-start
  946.0 7.7 copy-start.11
  992.3 5.7 copy-start
  998.0 7.7 copy-start.11
  1044.2 5.7 copy-start
  1050.0 7.7 copy-start.11
  1096.2 5.7 copy-start
  1102.0 7.7 copy-start.11
  1146.9 8.2 copy-start.33
  1155.1 4.5 copy-start.25
  1155.1 4.5 copy-start.26
  1155.1 4.5 copy-start.27
  1163.2 6.9 copy-start.35
  1163.2 6.9 copy-start.37
  1163.2 6.9 copy-start.39
  1163.2 6.9 copy-start.43
  1163.3 616.5 %all-reduce.7.cloned.1.call-start = ((), (), s32[]{:S(2)}) async-start(), calls=%async_computation.5 | async-start | bytes 16777216 | tf_op jit(solution)/shard_map/psum | solution.py:250
  1174.5 12.5 copy-start.63
  1174.5 33.4 %copy-start.13 = (f32[1,24,2,64,64]{4,3,2,1,0:T(8,128)S(1)}, f32[1,24,2,64,64]{4,3,2,1,0:T(8,128)}, u32[]{:S(2)}) copy-start(f32[1,24,2,64,64]{4,3,2,1,0:T(8,128)} %param.32) | copy-start | bytes 2359300
  1217.3 12.0 copy-start.16
  1381.4 146.4 %copy-start.55 = (pred[64,64]{1,0:T(8,128)(4,1)S(1)}, pred[64,64]{1,0:T(8,128)(4,1)}, u32[]{:S(2)}) copy-start(pred[64,64]{1,0:T(8,128)(4,1)} %iota_compare_fusion.3) | copy-start | bytes 12292
  1381.4 148.1 %copy-start.54 = (pred[64,64]{1,0:T(8,128)(4,1)S(1)}, pred[64,64]{1,0:T(8,128)(4,1)}, u32[]{:S(2)}) copy-start(pred[64,64]{1,0:T(8,128)(4,1)} %iota_compare_fusion.2) | copy-start | bytes 12292
  1385.5 392.4 %copy-start.19 = (f32[24,64,64]{1,2,0:T(8,128)S(1)}, f32[24,64,64]{1,2,0:T(8,128)}, u32[]{:S(2)}) copy-start(f32[24,64,64]{1,2,0:T(8,128)} %copy-done.18) | copy-start | bytes 1179652
  1385.5 392.4 %copy-start.21 = (f32[24,64,64]{1,2,0:T(8,128)S(1)}, f32[24,64,64]{1,2,0:T(8,128)}, u32[]{:S(2)}) copy-start(f32[24,64,64]{1,2,0:T(8,128)} %copy-done.20) | copy-start | bytes 1179652
  1773.5 6.2 copy-start.53
  1776.3 9.4 copy-start.50
  1776.3 9.5 copy-start.46
  1779.8 6.0 copy-start.4
  1779.8 6.0 copy-start.9
  1779.8 10.8 copy-start.56
  1779.8 23.5 %copy-start.59 = (f32[128]{0:T(128)S(1)}, f32[128]{0:T(128)}, u32[]{:S(2)}) copy-start(f32[128]{0:T(128)} %param.33) | copy-start | bytes 1540
  1779.8 23.5 %copy-start.60 = (f32[128]{0:T(128)S(1)}, f32[128]{0:T(128)}, u32[]{:S(2)}) copy-start(f32[128]{0:T(128)} %param.36) | copy-start | bytes 1540
  1779.8 23.5 %copy-start.61 = (f32[128]{0:T(128)S(1)}, f32[128]{0:T(128)}, u32[]{:S(2)}) copy-start(f32[128]{0:T(128)} %param.34) | copy-start | bytes 1540
  1779.8 23.5 %copy-start.62 = (f32[128]{0:T(128)S(1)}, f32[128]{0:T(128)}, u32[]{:S(2)}) copy-start(f32[128]{0:T(128)} %param.35) | copy-start | bytes 1540
  1779.8 24.1 %copy-start.48 = (f32[4096]{0:T(1024)S(1)}, f32[4096]{0:T(1024)}, u32[]{:S(2)}) copy-start(f32[4096]{0:T(1024)} %copy-done.47) | copy-start | bytes 49156
  (21 other events, 54.6 us)
Sparse Core Ops, SparseCore 0:
  10.5 35.0 all-gather.4
  208.6 154.9 all-reduce.4
  407.7 285.7 all-gather.6
  1163.4 44.4 reduce-scatter.1
  1210.9 291.6 all-reduce.6
